TPU v7x, 256 devices: a whole 4x4x8 slice. The times are simulated.
256 devices in a mesh: row: 8 (over x, core), col: 32 (over z, y).
Axes of the slice: x: 4, y: 4, z: 8, core: 2. Of those that a mesh axis runs over, the one named last changes fastest.
Arguments:
- blocks: bfloat16 [12288, 27, 48, 48], P(('row', 'col')), may hold values from -0.59765625 to 0.59765625
- prolong: bfloat16 [12288, 48, 48], P(('row', 'col')), may hold values from -0.875 to 0.875
- columns: int32 [12288, 27], P(('row', 'col')), may hold values from 0 to 383
- aggregate: int32 [12288], P(('row', 'col')), may hold values from 0 to 15
- slots: int32 [12288, 27], P(('row', 'col')), may hold values from 0 to 26
Outputs:
- coarse: float32 [128, 27, 2304], P('row', None, 'col')
Inputs may be any that keep to these rules, and one draw needn't show every extreme that they name: `columns`: a fine block row's neighbours all lie in its column tile: the fine block rows of the devices with the same col index, in order of their row index.
All inputs are finite; a program needn't handle non-finite values.
Results may differ from a plain program's by a relative error of at most 0.0029.
Values may be sent and summed in bfloat16 or wider, within the bound.
No kernel may reach another device: no remote copies, remote signals or barrier semaphores. Data moves between devices by JAX's collectives and lax.ppermute only.
A program may use at most 192 MiB of HBM per device.

v0:
```python
import jax
import jax.numpy as jnp
from jax import lax
from jax.sharding import PartitionSpec as P

KC = 27
CR_SLAB = 16


def shards(blocks, prolong, columns, aggregate, slots):
    width = blocks.shape[2]
    tile = lax.all_gather(prolong, "row", axis=0, tiled=True)
    picked = jnp.take(tile, columns, axis=0)
    product = jnp.einsum(
        "rkab,rkbc->rkac", blocks, picked, preferred_element_type=jnp.float32
    ).astype(jnp.bfloat16)
    term = jnp.einsum("rba,rkbc->rkac", prolong, product, preferred_element_type=jnp.float32)
    target = (aggregate[:, None] * KC + slots).reshape(-1)
    partial_value = jax.ops.segment_sum(
        term.reshape(-1, width * width), target, num_segments=CR_SLAB * KC
    )
    partial_value = partial_value.reshape(CR_SLAB, KC, width * width)
    summed = lax.psum(partial_value, "col")
    share = width * width // lax.axis_size("col")
    result = lax.dynamic_slice_in_dim(summed, lax.axis_index("col") * share, share, 2)
    return result


def solution(mesh):
    return jax.shard_map(
        shards,
        mesh=mesh,
        in_specs=(
            P(("row", "col"), None, None, None),
            P(("row", "col"), None, None),
            P(("row", "col"), None),
            P(("row", "col")),
            P(("row", "col"), None),
        ),
        out_specs=P("row", None, "col"),
        check_vma=False,
    )
```

profile of v0, /device:TPU:2, one launch (start us, length us, event | category | flops | bytes accessed | tf_op | source)
XLA Modules:
  0.0 371.9 jit_solution(16122000803956569116)
XLA Ops:
  6.5 0.0 all-gather.2.cloned.1.call-start
  6.5 0.7 all-gather.2.cloned.1.call-update
  7.3 0.0 all-reduce.2.cloned.1.call-start
  7.3 0.7 compare_select_fusion
  8.0 0.1 copy.14
  8.1 0.1 reshape.17
  8.2 0.7 compare_and_fusion
  9.0 0.1 copy.13
  9.1 0.7 broadcast_multiply_fusion
  9.7 0.7 broadcast_add_fusion
  10.4 0.1 copy.12
  10.5 0.1 reshape.25
  10.7 37.4 %all-gather.2.cloned.1.call-done = bf16[384,48,48]{2,1,0:T(8,128)(2,1)} async-done(((bf16[48,48,48]{2,1,0:T(8,128)(2,1)}), bf16[384,48,48]{2,1,0:T(8,128)(2,1)}) %all-gather.2.cloned.1.call-update) | async-done | bytes 1769488 | tf_op jit(solution)/shard_map/all_gather | solution.py:12
  48.0 10.4 %gather_fusion = bf16[1296,48,48]{2,1,0:T(8,128)(2,1)} fusion(bf16[384,48,48]{2,1,0:T(8,128)(2,1)} %all-gather.2.cloned.1.call-done, s32[2048]{0:T(1024)S(1)} %pad_clamp_fusion), kind=kCustom, calls=%fused_computation | custom fusion | bytes 11949120 | tf_op jit(solution)/shard_map/jit(_take)/gather | solution.py:13
  58.5 22.0 %copy.15 = bf16[48,27,48,48]{2,3,1,0:T(8,128)(2,1)} copy(bf16[48,27,48,48]{3,2,1,0:T(8,128)(2,1)} %bitcast.16) | data formatting | bytes 11943936 | tf_op jit(solution)/shard_map/jit(_take)/gather | solution.py:13
  80.4 27.9 %fusion.10 = f32[48,27,48,48]{2,3,1,0:T(8,128)} fusion(bf16[48,27,48,48]{3,2,1,0:T(8,128)(2,1)} %param.5, bf16[48,27,48,48]{2,3,1,0:T(8,128)(2,1)} %copy.15, pred[48,27]{1,0:T(8,128)(4,1)S(1)} %copy.13, bf16[48,48,48]{2,1,0:T(8,128)(2,1)S(1)} %copy-done), kind=kOutput, calls=%fused_computation.8 | convolution fusion | flops 579280896 | bytes 24110352 | tf_op jit(solution)/shard_map/rba,rkbc->rkac/dot_general | solution.py:17
  108.3 32.6 %copy.16 = f32[48,27,48,48]{3,2,1,0:T(8,128)} copy(f32[48,27,48,48]{2,3,1,0:T(8,128)} %fusion.10) | data formatting | bytes 23887872 | tf_op jit(solution)/shard_map/rba,rkbc->rkac/transpose | solution.py:17
  140.9 25.7 %reshape.27 = f32[1296,2304]{1,0:T(8,128)} reshape(f32[48,27,48,48]{3,2,1,0:T(8,128)} %copy.16) | data formatting | bytes 23887872 | tf_op jit(solution)/shard_map/reshape | solution.py:20
  166.6 24.2 %scatter_custom_fusion = f32[432,2304]{1,0:T(8,128)} fusion(s32[1296]{0:T(1024)S(1)} %reshape.25, f32[1296,2304]{1,0:T(8,128)} %reshape.27, f32[]{:T(128)} %constant.9.clone.1), kind=kCustom, calls=%fused_computation.10 | custom fusion | flops 2985984 | bytes 3981824 | tf_op jit(solution)/shard_map/scatter-add | solution.py:19
  190.8 3.9 %reshape.14 = f32[16,27,2304]{2,1,0:T(8,128)} reshape(f32[432,2304]{1,0:T(8,128)} %scatter_custom_fusion) | data formatting | bytes 7962624 | tf_op jit(solution)/shard_map/reshape | solution.py:22
  194.7 0.0 all-reduce.2.cloned.1.call-update
  194.8 168.3 %all-reduce.2.cloned.1.call-done = f32[16,27,2304]{2,1,0:T(8,128)} async-done(((f32[16,27,2304]{2,1,0:T(8,128)}), f32[16,27,2304]{2,1,0:T(8,128)}) %all-reduce.2.cloned.1.call-update) | async-done | bytes 3981328 | tf_op jit(solution)/shard_map/psum | solution.py:23
  363.1 1.2 constant_dynamic-slice_fusion
  364.3 0.8 copy.17
  (3 shorter events, 0.0 us)
Async XLA Ops:
  6.5 41.5 %all-gather.2.cloned.1.call-start = ((), (), s32[]{:S(2)}) async-start(), calls=%async_computation | async-start | bytes 5308416 | tf_op jit(solution)/shard_map/all_gather | solution.py:12
  7.3 355.8 %all-reduce.2.cloned.1.call-start = ((), (), s32[]{:S(2)}) async-start(), calls=%async_computation.1 | async-start | bytes 9437184 | tf_op jit(solution)/shard_map/psum | solution.py:23
  58.5 22.0 %copy-start = (bf16[48,48,48]{2,1,0:T(8,128)(2,1)S(1)}, bf16[48,48,48]{2,1,0:T(8,128)(2,1)}, u32[]{:S(2)}) copy-start(bf16[48,48,48]{2,1,0:T(8,128)(2,1)} %param.6) | copy-start | bytes 663556
Sparse Core Ops, SparseCore 0:
  9.2 38.8 all-gather.1
  194.9 168.1 all-reduce.1
where the time goes:
time: 374 us; the launch traced here: 372 us
  waiting for transfers between devices  206 us (55%)
  local copies, waits for them, and re-layouts  97.1 us (26%)
  matrix products  27.9 us (7%)
  other arithmetic  27.1 us (7%)
  between operations  13.4 us (4%)
    psum x1, waiting for transfers between devices, shards(): summed = lax.psum(partial_value, 'col')  168 us
    all_gather x1, waiting for transfers between devices, shards(): tile = lax.all_gather(prolong, 'row', axis=0, tiled=True)  37.4 us
    transpose x1, local copies, waits for them, and re-layouts, shards(): jnp.einsum('rba,rkbc->rkac', prolong, product, preferred_element_type=jnp...  32.6 us
    gather x2, local copies, waits for them, and re-layouts, shards(): picked = jnp.take(tile, columns, axis=0)  32.4 us
    dot_general x1, matrix products, shards(): jnp.einsum('rba,rkbc->rkac', prolong, product, preferred_element_type=jnp...  27.9 us
    reshape x1, local copies, waits for them, and re-layouts, shards(): term.reshape(-1, width * width)  25.7 us
    scatter-add x1, other arithmetic, shards(): jax.ops.segment_sum(term.reshape(-1, width * width), target, num_segments...  24.2 us
  transfers between devices with their start and end apart: 2, of which 2 were waited for; matrix products, arithmetic and copies ran while one was open for 1% of the time, Pallas kernels for 0%

commit v1 on v0

--- a/solution.py
+++ b/solution.py
@@ -20,7 +20,9 @@
         term.reshape(-1, width * width), target, num_segments=CR_SLAB * KC
     )
     partial_value = partial_value.reshape(CR_SLAB, KC, width * width)
-    summed = lax.psum(partial_value, "col")
+    summed = partial_value
+    for hop in (1, 2, 4, 8, 16):
+        summed = summed + lax.ppermute(summed, "col", [(dev, dev ^ hop) for dev in range(32)])
     share = width * width // lax.axis_size("col")
     result = lax.dynamic_slice_in_dim(summed, lax.axis_index("col") * share, share, 2)
     return result

time: 374 us -> 834 us (2.23)
  waiting for transfers between devices: 206 us -> 637 us
  starting transfers between devices: 0.04 us -> 14.9 us
  other arithmetic: 27.1 us -> 37.3 us
    ppermute x0 -> x5, waiting for transfers between devices: none -> 599 us  [shards(): lax.ppermute(summed, 'col', [(dev, dev ^ hop) for dev in range(32)])]
    psum x1 -> x0, waiting for transfers between devices: 168 us -> none  [shards(): summed = lax.psum(partial_value, 'col')]
    ppermute x0 -> x5, starting transfers between devices: none -> 14.9 us  [shards(): lax.ppermute(summed, 'col', [(dev, dev ^ hop) for dev in range(32)])]
    add x0 -> x5, other arithmetic: none -> 10.3 us  [shards(): summed + lax.ppermute(summed, 'col', [(dev, dev ^ hop) for dev in range(3...]
  transfers between devices with their start and end apart: 2 -> 6, of which waited for: 2 -> 6; matrix products, arithmetic and copies ran while one was open for 1% -> 0% of each run, Pallas kernels for 0% -> 0%
where the time goes in v1:
time: 834 us; the launch traced here: 830 us
  waiting for transfers between devices  637 us (76%)
  local copies, waits for them, and re-layouts  99.7 us (12%)
  other arithmetic  37.3 us (4%)
  matrix products  27.9 us (3%)
  starting transfers between devices  14.9 us (2%)
  between operations  13.4 us (2%)
    ppermute x5, waiting for transfers between devices, shards(): lax.ppermute(summed, 'col', [(dev, dev ^ hop) for dev in range(32)])  599 us
    all_gather x1, waiting for transfers between devices, shards(): tile = lax.all_gather(prolong, 'row', axis=0, tiled=True)  37.4 us
    transpose x1, local copies, waits for them, and re-layouts, shards(): jnp.einsum('rba,rkbc->rkac', prolong, product, preferred_element_type=jnp...  32.6 us
    gather x2, local copies, waits for them, and re-layouts, shards(): picked = jnp.take(tile, columns, axis=0)  32.4 us
    dot_general x1, matrix products, shards(): jnp.einsum('rba,rkbc->rkac', prolong, product, preferred_element_type=jnp...  27.9 us
    reshape x1, local copies, waits for them, and re-layouts, shards(): term.reshape(-1, width * width)  25.7 us
    scatter-add x1, other arithmetic, shards(): jax.ops.segment_sum(term.reshape(-1, width * width), target, num_segments...  24.2 us
  transfers between devices with their start and end apart: 6, of which 6 were waited for; matrix products, arithmetic and copies ran while one was open for 0% of the time, Pallas kernels for 0%

profile of v1, /device:TPU:2, one launch (start us, length us, event | category | flops | bytes accessed | tf_op | source)
XLA Modules:
  0.0 830.5 jit_solution(6747766278406838693)
XLA Ops:
  7.3 0.7 compare_select_fusion
  8.2 0.7 compare_and_fusion
  10.6 37.4 %all-gather.2.cloned.1.call-done = bf16[384,48,48]{2,1,0:T(8,128)(2,1)} async-done(((bf16[48,48,48]{2,1,0:T(8,128)(2,1)}), bf16[384,48,48]{2,1,0:T(8,128)(2,1)}) %all-gather.2.cloned.1.call-update) | async-done | bytes 1769488 | tf_op jit(solution)/shard_map/all_gather | solution.py:12
  48.0 10.4 %gather_fusion = bf16[1296,48,48]{2,1,0:T(8,128)(2,1)} fusion(bf16[384,48,48]{2,1,0:T(8,128)(2,1)} %all-gather.2.cloned.1.call-done, s32[2048]{0:T(1024)S(1)} %pad_clamp_fusion), kind=kCustom, calls=%fused_computation | custom fusion | bytes 11949120 | tf_op jit(solution)/shard_map/jit(_take)/gather | solution.py:13
  58.5 21.9 %copy.31 = bf16[48,27,48,48]{2,3,1,0:T(8,128)(2,1)} copy(bf16[48,27,48,48]{3,2,1,0:T(8,128)(2,1)} %bitcast.16) | data formatting | bytes 11943936 | tf_op jit(solution)/shard_map/jit(_take)/gather | solution.py:13
  80.4 27.9 %fusion.10 = f32[48,27,48,48]{2,3,1,0:T(8,128)} fusion(bf16[48,27,48,48]{3,2,1,0:T(8,128)(2,1)} %param.5, bf16[48,27,48,48]{2,3,1,0:T(8,128)(2,1)} %copy.31, pred[48,27]{1,0:T(8,128)(4,1)S(1)} %copy.29, bf16[48,48,48]{2,1,0:T(8,128)(2,1)S(1)} %copy-done), kind=kOutput, calls=%fused_computation.8 | convolution fusion | flops 579280896 | bytes 24110352 | tf_op jit(solution)/shard_map/rba,rkbc->rkac/dot_general | solution.py:17
  108.3 32.6 %copy.32 = f32[48,27,48,48]{3,2,1,0:T(8,128)} copy(f32[48,27,48,48]{2,3,1,0:T(8,128)} %fusion.10) | data formatting | bytes 23887872 | tf_op jit(solution)/shard_map/rba,rkbc->rkac/transpose | solution.py:17
  140.9 25.7 %reshape.27 = f32[1296,2304]{1,0:T(8,128)} reshape(f32[48,27,48,48]{3,2,1,0:T(8,128)} %copy.32) | data formatting | bytes 23887872 | tf_op jit(solution)/shard_map/reshape | solution.py:20
  166.5 24.2 %scatter_custom_fusion = f32[432,2304]{1,0:T(8,128)} fusion(s32[1296]{0:T(1024)S(1)} %reshape.25, f32[1296,2304]{1,0:T(8,128)} %reshape.27, f32[]{:T(128)} %constant.9.clone.1), kind=kCustom, calls=%fused_computation.10 | custom fusion | flops 2985984 | bytes 3981824 | tf_op jit(solution)/shard_map/scatter-add | solution.py:19
  190.8 3.9 reshape.14
  194.7 4.6 copy.34
  199.4 1.8 collective-permute-start
  201.1 86.7 %collective-permute-done = f32[16,27,2304]{2,0,1:T(8,128)S(1)} collective-permute-done((f32[16,27,2304]{2,0,1:T(8,128)S(1)}, f32[16,27,2304]{2,0,1:T(8,128)S(1)}, u32[]{:S(2)}, u32[]{:S(2)}) %collective-permute-start) | collective-permute-done | bytes 3981344 | tf_op jit(solution)/shard_map/ppermute | solution.py:25
  287.8 5.1 copy_add_fusion
  292.9 3.1 collective-permute-start.1
  296.0 85.8 %collective-permute-done.1 = f32[16,27,2304]{2,0,1:T(8,128)S(1)} collective-permute-done((f32[16,27,2304]{2,0,1:T(8,128)S(1)}, f32[16,27,2304]{2,0,1:T(8,128)S(1)}, u32[]{:S(2)}, u32[]{:S(2)}) %collective-permute-start.1) | collective-permute-done | bytes 3981344 | tf_op jit(solution)/shard_map/ppermute | solution.py:25
  382.3 1.6 collective-permute-start.2
  383.9 84.9 %collective-permute-done.2 = f32[16,27,2304]{2,0,1:T(8,128)S(1)} collective-permute-done((f32[16,27,2304]{2,0,1:T(8,128)S(1)}, f32[16,27,2304]{2,0,1:T(8,128)S(1)}, u32[]{:S(2)}, u32[]{:S(2)}) %collective-permute-start.2) | collective-permute-done | bytes 3981344 | tf_op jit(solution)/shard_map/ppermute | solution.py:25
  469.2 2.6 collective-permute-start.3
  471.8 169.2 %collective-permute-done.3 = f32[16,27,2304]{2,0,1:T(8,128)S(1)} collective-permute-done((f32[16,27,2304]{2,0,1:T(8,128)S(1)}, f32[16,27,2304]{2,0,1:T(8,128)S(1)}, u32[]{:S(2)}, u32[]{:S(2)}) %collective-permute-start.3) | collective-permute-done | bytes 3981344 | tf_op jit(solution)/shard_map/ppermute | solution.py:25
  641.0 2.3 add.43
  643.3 5.7 collective-permute-start.4
  649.0 172.6 %collective-permute-done.4 = f32[16,27,2304]{2,0,1:T(8,128)} collective-permute-done((f32[16,27,2304]{2,0,1:T(8,128)}, f32[16,27,2304]{2,0,1:T(8,128)}, u32[]{:S(2)}, u32[]{:S(2)}) %collective-permute-start.4) | collective-permute-done | bytes 3981344 | tf_op jit(solution)/shard_map/ppermute | solution.py:25
  821.6 2.0 dynamic-slice_add_fusion
  (14 shorter events, 3.5 us)
Async XLA Ops:
  6.5 41.5 %all-gather.2.cloned.1.call-start = ((), (), s32[]{:S(2)}) async-start(), calls=%async_computation | async-start | bytes 5308416 | tf_op jit(solution)/shard_map/all_gather | solution.py:12
  58.5 21.9 %copy-start = (bf16[48,48,48]{2,1,0:T(8,128)(2,1)S(1)}, bf16[48,48,48]{2,1,0:T(8,128)(2,1)}, u32[]{:S(2)}) copy-start(bf16[48,48,48]{2,1,0:T(8,128)(2,1)} %param.6) | copy-start | bytes 663556
  199.4 88.5 %collective-permute-start = (f32[16,27,2304]{2,0,1:T(8,128)S(1)}, f32[16,27,2304]{2,0,1:T(8,128)S(1)}, u32[]{:S(2)}, u32[]{:S(2)}) collective-permute-start(f32[16,27,2304]{2,0,1:T(8,128)S(1)} %copy.34), channel_id=1, source_target_pairs={{0,1},{1,0},{2,3},{3,2},{4,5},{5,4},{6,7},{7,6},{8,9},{9,8},{10,11... | collective-permute-start | bytes 11943944 | tf_op jit(solution)/shard_map/ppermute | solution.py:25
  292.9 88.9 %collective-permute-start.1 = (f32[16,27,2304]{2,0,1:T(8,128)S(1)}, f32[16,27,2304]{2,0,1:T(8,128)S(1)}, u32[]{:S(2)}, u32[]{:S(2)}) collective-permute-start(f32[16,27,2304]{2,0,1:T(8,128)S(1)} %copy_add_fusion), channel_id=1, source_target_pairs={{0,2},{1,3},{2,0},{3,1},{4,6},{5,7},{6,4},{7,5},{8,10},{9,11},{10,... | collective-permute-start | bytes 11943944 | tf_op jit(solution)/shard_map/ppermute | solution.py:25
  382.3 86.5 %collective-permute-start.2 = (f32[16,27,2304]{2,0,1:T(8,128)S(1)}, f32[16,27,2304]{2,0,1:T(8,128)S(1)}, u32[]{:S(2)}, u32[]{:S(2)}) collective-permute-start(f32[16,27,2304]{2,0,1:T(8,128)S(1)} %add.41), channel_id=1, source_target_pairs={{0,4},{1,5},{2,6},{3,7},{4,0},{5,1},{6,2},{7,3},{8,12},{9,13},{10,... | collective-permute-start | bytes 11943944 | tf_op jit(solution)/shard_map/ppermute | solution.py:25
  469.2 171.8 %collective-permute-start.3 = (f32[16,27,2304]{2,0,1:T(8,128)S(1)}, f32[16,27,2304]{2,0,1:T(8,128)S(1)}, u32[]{:S(2)}, u32[]{:S(2)}) collective-permute-start(f32[16,27,2304]{2,0,1:T(8,128)S(1)} %add.42), channel_id=1, source_target_pairs={{0,8},{1,9},{2,10},{3,11},{4,12},{5,13},{6,14},{7,15},{8,0},{9,1},... | collective-permute-start | bytes 11943944 | tf_op jit(solution)/shard_map/ppermute | solution.py:25
  643.3 178.3 %collective-permute-start.4 = (f32[16,27,2304]{2,0,1:T(8,128)}, f32[16,27,2304]{2,0,1:T(8,128)}, u32[]{:S(2)}, u32[]{:S(2)}) collective-permute-start(f32[16,27,2304]{2,0,1:T(8,128)} %add.43), channel_id=1, source_target_pairs={{0,16},{1,17},{2,18},{3,19},{4,20},{5,21},{6,22},{7,23},{8,24},{9,... | collective-permute-start | bytes 11943944 | tf_op jit(solution)/shard_map/ppermute | solution.py:25
Sparse Core Ops, SparseCore 0:
  9.2 38.8 all-gather.1
